TPU v7x, 256 devices: a whole 4x4x8 slice. The times are simulated.
256 devices in a mesh: section: 4 (over x), dp: 16 (over y_hi, z), tensor: 4 (over y_lo, core).
Axes of the slice: x: 4, y: 4 (y_hi: 2, y_lo: 2; y = y_hi * 2 + y_lo), z: 8, core: 2. Of those that a mesh axis runs over, the one named last changes fastest.
Arguments:
- enc_input: bfloat16 [2, 16, 128, 4096], P(None, 'dp', None, 'tensor'), may hold values from -10.8 to 10.8
- dec_input: bfloat16 [2, 16, 128, 4096], P(None, 'dp', None, 'tensor'), may hold values from -6 to 6
- lengths: int32 [2, 2, 16], P(None, None, 'dp'), may hold values from 16 to 128, as said below
- offset_bucket: int32 [2, 255], replicated, may hold values from 0 to 31
- bias_tables: float32 [2, 32, 32], P(None, None, 'tensor'), may hold values from -4.5 to 303
- norm_gain: float32 [4, 4096], P('section'), may hold values from 0.5 to 1.5
- final_gain: float32 [4096], P('tensor'), may hold values from 0.5 to 1.5
- w_query: bfloat16 [4, 4096, 2048], P('section', 'dp', 'tensor'), may hold values from -0.0234375 to 0.0234375
- w_key: bfloat16 [4, 4096, 2048], P('section', 'dp', 'tensor'), may hold values from -0.09375 to 0.09375
- w_value: bfloat16 [4, 4096, 2048], P('section', 'dp', 'tensor'), may hold values from -0.09375 to 0.09375
- w_out: bfloat16 [4, 2048, 4096], P('section', 'tensor', 'dp'), may hold values from -0.125 to 0.125
Outputs:
- section_out: bfloat16 [4, 2, 16, 128, 4096], P('section', None, 'dp', None, 'tensor')
Inputs may be any that keep to these rules, and one draw needn't show every extreme that they name: In every micro-batch, sequence 0 has both lengths equal to 128.
All inputs are finite; a program needn't handle non-finite values.
Results may differ from a plain program's by a relative error of at most 0.02.
Values may be sent and summed in bfloat16 or wider, within the bound.
No kernel may reach another device: no remote copies, remote signals or barrier semaphores. Data moves between devices by JAX's collectives and lax.ppermute only.
A program may use at most 128 MiB of HBM per device.

v0:
```python
import jax
import jax.numpy as jnp
from jax import lax
from jax.sharding import PartitionSpec as P

D = 4096
HEAD_DIM = 64


def shifted(value, axis, steps):
    count = lax.axis_size(axis)
    initial, last = (max(0, -steps), min(count, count - steps))
    return lax.ppermute(value, axis, [(source, source + steps) for source in range(initial, last)])


def positional_bias(offset_bucket, bias_tables, section_id, length):
    bucket_row = jnp.where(section_id == 0, offset_bucket[0], offset_bucket[1])
    tables = jnp.where(section_id == 0, bias_tables[0], bias_tables[1])
    tables = tables * jnp.where(section_id == 2, 0.0, 1.0).astype(jnp.float32)
    query_pos = lax.broadcasted_iota(jnp.int32, (length, length), 0)
    key_pos = lax.broadcasted_iota(jnp.int32, (length, length), 1)
    bucket = jnp.take(bucket_row, key_pos - query_pos + (length - 1))
    bucket_ids = lax.broadcasted_iota(jnp.int32, (1, 1, tables.shape[0]), 2)
    onehot = (bucket[:, :, None] == bucket_ids).astype(jnp.float32)
    return jnp.einsum("qkb,bh->hqk", onehot, tables, precision=lax.Precision.HIGHEST)


def attend_local(
    layer_normed,
    encoder_memory,
    complete_query,
    complete_key,
    complete_value,
    complete_output,
    score_bias,
    allowed,
):
    seq_count, length, width = layer_normed.shape
    queries = jnp.einsum(
        "vyt,te->vye", layer_normed, complete_query, preferred_element_type=jnp.float32
    ).astype(jnp.bfloat16)
    keys_proj = jnp.einsum(
        "vyt,te->vye", encoder_memory, complete_key, preferred_element_type=jnp.float32
    ).astype(jnp.bfloat16)
    values = jnp.einsum(
        "vyt,te->vye", encoder_memory, complete_value, preferred_element_type=jnp.float32
    ).astype(jnp.bfloat16)
    head_count = queries.shape[2] // HEAD_DIM
    query_heads = queries.reshape(seq_count, length, head_count, HEAD_DIM)
    key_heads = keys_proj.reshape(seq_count, length, head_count, HEAD_DIM)
    value_heads = values.reshape(seq_count, length, head_count, HEAD_DIM)
    scores = jnp.einsum(
        "sqhc,skhc->shqk", query_heads, key_heads, preferred_element_type=jnp.float32
    )
    scores = scores + score_bias[None]
    scores = jnp.where(allowed[:, None], scores, -1e30)
    highest = jnp.max(scores, axis=-1, keepdims=True)
    expsum = jnp.exp(scores - highest)
    weights_bf = (expsum / jnp.sum(expsum, axis=-1, keepdims=True)).astype(jnp.bfloat16)
    attended_context = jnp.einsum(
        "shqk,skhc->sqhc", weights_bf, value_heads, preferred_element_type=jnp.float32
    ).astype(jnp.bfloat16)
    attended_context = attended_context.reshape(seq_count, length, head_count * HEAD_DIM)
    return jnp.einsum(
        "bqf,fw->bqw", attended_context, complete_output, preferred_element_type=jnp.float32
    )


def body(
    enc_input,
    dec_input,
    lengths,
    offset_bucket,
    bias_tables,
    norm_gain,
    final_gain,
    w_query,
    w_key,
    w_value,
    w_out,
):
    section_id = lax.axis_index("section")
    micro_count, seq_count, length, quarter = enc_input.shape
    complete_query, complete_key, complete_value, complete_output = (
        lax.all_gather(w_query[0], "dp", axis=0, tiled=True),
        lax.all_gather(w_key[0], "dp", axis=0, tiled=True),
        lax.all_gather(w_value[0], "dp", axis=0, tiled=True),
        lax.all_gather(w_out[0], "dp", axis=1, tiled=True),
    )
    score_bias = positional_bias(offset_bucket, bias_tables, section_id, length)
    query_pos = lax.broadcasted_iota(jnp.int32, (length, length), 0)
    key_pos = lax.broadcasted_iota(jnp.int32, (length, length), 1)
    causal = jnp.logical_or(section_id == 1, section_id == 3)
    encoder_keys = jnp.logical_or(section_id == 0, section_id == 2)
    order_ok = jnp.logical_or(jnp.logical_not(causal), key_pos <= query_pos)
    gain_full = norm_gain[0]
    tick_count = micro_count + lax.axis_size("section") - 1
    zero_block = jnp.zeros((seq_count, length, quarter), jnp.bfloat16)
    carry_h = zero_block
    carry_e = zero_block
    record = jnp.zeros((micro_count, seq_count, length, quarter), jnp.bfloat16)
    for moment in range(tick_count):
        offset = moment - section_id
        active = jnp.logical_and(offset >= 0, offset < micro_count)
        micro_id = jnp.clip(offset, 0, micro_count - 1)
        enc_now = lax.dynamic_index_in_dim(enc_input, micro_id, 0, keepdims=False)
        dec_now = lax.dynamic_index_in_dim(dec_input, micro_id, 0, keepdims=False)
        input_rows = jnp.where(
            section_id == 0, enc_now, jnp.where(section_id == 1, dec_now, carry_h)
        )
        length_pair = lax.dynamic_index_in_dim(lengths, micro_id, 0, keepdims=False)
        key_len = jnp.where(encoder_keys, length_pair[0], length_pair[1])
        allowed = jnp.logical_and(key_pos[None] < key_len[:, None, None], order_ok[None])
        memory_part = carry_e
        gathered, memory_whole = (
            lax.all_gather(input_rows, "tensor", axis=2, tiled=True),
            lax.all_gather(memory_part, "tensor", axis=2, tiled=True),
        )
        single = gathered.astype(jnp.float32)
        mean_sq = jnp.mean(single * single, axis=-1, keepdims=True)
        layer_normed = (single * lax.rsqrt(mean_sq + 1e-06) * gain_full).astype(jnp.bfloat16)
        encoder_memory = jnp.where(section_id == 2, memory_whole, layer_normed)
        partial_value = attend_local(
            layer_normed,
            encoder_memory,
            complete_query,
            complete_key,
            complete_value,
            complete_output,
            score_bias,
            allowed,
        )
        shared = lax.psum_scatter(
            partial_value.astype(jnp.bfloat16), "tensor", scatter_dimension=2, tiled=True
        ).astype(jnp.float32)
        hidden_wide = input_rows.astype(jnp.float32) + shared
        hidden = hidden_wide.astype(jnp.bfloat16)
        hidden_back = hidden.astype(jnp.float32)
        enc_square = lax.psum(jnp.sum(hidden_back * hidden_back, axis=-1), "tensor")
        enc_out = (hidden_back * lax.rsqrt(enc_square / D + 1e-06)[:, :, None] * final_gain).astype(
            jnp.bfloat16
        )
        result = jnp.where(section_id == 0, enc_out, hidden)
        current = lax.dynamic_index_in_dim(record, micro_id, 0, keepdims=False)
        record = lax.dynamic_update_index_in_dim(
            record, jnp.where(active, result, current), micro_id, 0
        )
        if moment + 1 < tick_count:
            enc_pass = jnp.where(section_id == 0, enc_out, carry_e)
            carry_h, carry_e = shifted((result, enc_pass), "section", 1)
    return record[None]


def solution(mesh):
    in_specs = (
        P(None, "dp", None, "tensor"),
        P(None, "dp", None, "tensor"),
        P(None, None, "dp"),
        P(),
        P(None, None, "tensor"),
        P("section", None),
        P("tensor"),
        P("section", "dp", "tensor"),
        P("section", "dp", "tensor"),
        P("section", "dp", "tensor"),
        P("section", "tensor", "dp"),
    )
    out_specs = P("section", None, "dp", None, "tensor")
    return jax.shard_map(body, mesh=mesh, in_specs=in_specs, out_specs=out_specs, check_vma=False)
```

profile of v0, /device:TPU:1, one launch (start us, length us, event | category | flops | bytes accessed | tf_op | source)
XLA Modules:
  0.0 913.5 jit_solution(5208827000141781013)
XLA Ops:
  11.1 101.4 %gather_fusion = s32[16384]{0:T(1024)S(1)} fusion(s32[255]{0:T(256)S(1)} %bitcast.319, s32[16384]{0:T(1024)S(1)} %fusion.172), kind=kCustom, calls=%fused_computation | custom fusion | bytes 196608 | tf_op jit(solution)/shard_map/jit(_take)/gather | solution.py:22
  117.2 18.8 %all-gather.37.cloned.1.call-done = bf16[1,4096,512]{2,1,0:T(8,128)(2,1)} async-done(((bf16[1,256,512]{2,1,0:T(8,128)(2,1)}), bf16[1,4096,512]{2,1,0:T(8,128)(2,1)}) %all-gather.37.cloned.1.call-update) | async-done | bytes 4194320 | tf_op jit(solution)/shard_map/all_gather | solution.py:87
  139.5 95.5 %all-gather.39.cloned.1.call-done = bf16[1,4096,512]{2,1,0:T(8,128)(2,1)} async-done(((bf16[1,256,512]{2,1,0:T(8,128)(2,1)}), bf16[1,4096,512]{2,1,0:T(8,128)(2,1)}) %all-gather.39.cloned.1.call-update) | async-done | bytes 4194320 | tf_op jit(solution)/shard_map/all_gather | solution.py:85
  238.1 95.7 %all-gather.41.cloned.1.call-done = bf16[1,4096,512]{2,1,0:T(8,128)(2,1)} async-done(((bf16[1,256,512]{2,1,0:T(8,128)(2,1)}), bf16[1,4096,512]{2,1,0:T(8,128)(2,1)}) %all-gather.41.cloned.1.call-update) | async-done | bytes 4194320 | tf_op jit(solution)/shard_map/all_gather | solution.py:86
  337.6 100.2 %all-gather.43.cloned.1.call-done = bf16[1,512,4096]{2,1,0:T(8,128)(2,1)} async-done(((bf16[1,512,256]{2,1,0:T(8,128)(2,1)}), bf16[1,512,4096]{2,1,0:T(8,128)(2,1)}) %all-gather.43.cloned.1.call-update) | async-done | bytes 4194320 | tf_op jit(solution)/shard_map/all_gather | solution.py:88
  437.8 4.0 fusion.5
  441.9 23.7 %reduce-scatter.6.cloned.1.call-done = bf16[1,128,1024]{2,1,0:T(8,128)(2,1)} async-done(((bf16[1,128,4096]{2,1,0:T(8,128)(2,1)}), bf16[1,128,1024]{2,1,0:T(8,128)(2,1)}) %reduce-scatter.6.cloned.1.call-update) | async-done | bytes 262160 | tf_op jit(solution)/shard_map/reduce_scatter | solution.py:133
  466.7 5.1 psum.35
  476.2 4.3 collective-permute-done
  481.5 4.1 collective-permute-start.1
  492.2 16.3 %all-gather.21.cloned.1.call-done = bf16[1,128,4096]{2,1,0:T(8,128)(2,1)} async-done(((bf16[1,128,1024]{2,1,0:T(8,128)(2,1)}), bf16[1,128,4096]{2,1,0:T(8,128)(2,1)}) %all-gather.21.cloned.1.call-update) | async-done | bytes 1048592 | tf_op jit(solution)/shard_map/all_gather | solution.py:116
  510.1 24.4 %all-gather.19.cloned.1.call-done = bf16[1,128,4096]{2,1,0:T(8,128)(2,1)} async-done(((bf16[1,128,1024]{2,1,0:T(8,128)(2,1)}), bf16[1,128,4096]{2,1,0:T(8,128)(2,1)}) %all-gather.19.cloned.1.call-update) | async-done | bytes 1048592 | tf_op jit(solution)/shard_map/all_gather | solution.py:117
  549.6 24.5 %reduce-scatter.8.cloned.1.call-done = bf16[1,128,1024]{2,1,0:T(8,128)(2,1)} async-done(((bf16[1,128,4096]{2,1,0:T(8,128)(2,1)}), bf16[1,128,1024]{2,1,0:T(8,128)(2,1)}) %reduce-scatter.8.cloned.1.call-update) | async-done | bytes 262160 | tf_op jit(solution)/shard_map/reduce_scatter | solution.py:133
  575.3 5.1 psum.36
  584.7 4.3 collective-permute-done.2
  590.0 4.1 collective-permute-start.3
  600.3 16.8 %all-gather.25.cloned.1.call-done = bf16[1,128,4096]{2,1,0:T(8,128)(2,1)} async-done(((bf16[1,128,1024]{2,1,0:T(8,128)(2,1)}), bf16[1,128,4096]{2,1,0:T(8,128)(2,1)}) %all-gather.25.cloned.1.call-update) | async-done | bytes 1048592 | tf_op jit(solution)/shard_map/all_gather | solution.py:116
  618.6 24.4 %all-gather.23.cloned.1.call-done = bf16[1,128,4096]{2,1,0:T(8,128)(2,1)} async-done(((bf16[1,128,1024]{2,1,0:T(8,128)(2,1)}), bf16[1,128,4096]{2,1,0:T(8,128)(2,1)}) %all-gather.23.cloned.1.call-update) | async-done | bytes 1048592 | tf_op jit(solution)/shard_map/all_gather | solution.py:117
  658.1 24.5 %reduce-scatter.10.cloned.1.call-done = bf16[1,128,1024]{2,1,0:T(8,128)(2,1)} async-done(((bf16[1,128,4096]{2,1,0:T(8,128)(2,1)}), bf16[1,128,1024]{2,1,0:T(8,128)(2,1)}) %reduce-scatter.10.cloned.1.call-update) | async-done | bytes 262160 | tf_op jit(solution)/shard_map/reduce_scatter | solution.py:133
  683.8 5.1 psum.37
  693.2 4.3 collective-permute-done.4
  698.6 4.1 collective-permute-start.5
  709.3 16.3 %all-gather.29.cloned.1.call-done = bf16[1,128,4096]{2,1,0:T(8,128)(2,1)} async-done(((bf16[1,128,1024]{2,1,0:T(8,128)(2,1)}), bf16[1,128,4096]{2,1,0:T(8,128)(2,1)}) %all-gather.29.cloned.1.call-update) | async-done | bytes 1048592 | tf_op jit(solution)/shard_map/all_gather | solution.py:116
  727.1 24.3 %all-gather.27.cloned.1.call-done = bf16[1,128,4096]{2,1,0:T(8,128)(2,1)} async-done(((bf16[1,128,1024]{2,1,0:T(8,128)(2,1)}), bf16[1,128,4096]{2,1,0:T(8,128)(2,1)}) %all-gather.27.cloned.1.call-update) | async-done | bytes 1048592 | tf_op jit(solution)/shard_map/all_gather | solution.py:117
  766.5 24.5 %reduce-scatter.12.cloned.1.call-done = bf16[1,128,1024]{2,1,0:T(8,128)(2,1)} async-done(((bf16[1,128,4096]{2,1,0:T(8,128)(2,1)}), bf16[1,128,1024]{2,1,0:T(8,128)(2,1)}) %reduce-scatter.12.cloned.1.call-update) | async-done | bytes 262160 | tf_op jit(solution)/shard_map/reduce_scatter | solution.py:133
  792.2 5.1 psum.38
  801.6 4.3 collective-permute-done.6
  806.9 4.1 collective-permute-start.7
  816.7 17.3 %all-gather.33.cloned.1.call-done = bf16[1,128,4096]{2,1,0:T(8,128)(2,1)} async-done(((bf16[1,128,1024]{2,1,0:T(8,128)(2,1)}), bf16[1,128,4096]{2,1,0:T(8,128)(2,1)}) %all-gather.33.cloned.1.call-update) | async-done | bytes 1048592 | tf_op jit(solution)/shard_map/all_gather | solution.py:116
  835.5 24.3 %all-gather.31.cloned.1.call-done = bf16[1,128,4096]{2,1,0:T(8,128)(2,1)} async-done(((bf16[1,128,1024]{2,1,0:T(8,128)(2,1)}), bf16[1,128,4096]{2,1,0:T(8,128)(2,1)}) %all-gather.31.cloned.1.call-update) | async-done | bytes 1048592 | tf_op jit(solution)/shard_map/all_gather | solution.py:117
  874.8 23.8 %reduce-scatter.14.cloned.1.call-done = bf16[1,128,1024]{2,1,0:T(8,128)(2,1)} async-done(((bf16[1,128,4096]{2,1,0:T(8,128)(2,1)}), bf16[1,128,1024]{2,1,0:T(8,128)(2,1)}) %reduce-scatter.14.cloned.1.call-update) | async-done | bytes 262160 | tf_op jit(solution)/shard_map/reduce_scatter | solution.py:133
  899.7 5.1 psum.39
  (209 shorter events, 132.5 us)
Async XLA Ops:
  6.5 109.1 %all-gather.35.cloned.1.call-start = ((), (), s32[]{:S(2)}) async-start(), calls=%async_computation.18 | async-start | bytes 1310720 | tf_op jit(solution)/shard_map/all_gather | solution.py:116
  8.3 127.7 %all-gather.37.cloned.1.call-start = ((), (), s32[]{:S(2)}) async-start(), calls=%async_computation.19 | async-start | bytes 4456448 | tf_op jit(solution)/shard_map/all_gather | solution.py:87
  9.1 225.9 %all-gather.39.cloned.1.call-start = ((), (), s32[]{:S(2)}) async-start(), calls=%async_computation.20 | async-start | bytes 4456448 | tf_op jit(solution)/shard_map/all_gather | solution.py:85
  9.8 324.0 %all-gather.41.cloned.1.call-start = ((), (), s32[]{:S(2)}) async-start(), calls=%async_computation.21 | async-start | bytes 4456448 | tf_op jit(solution)/shard_map/all_gather | solution.py:86
  10.4 427.4 %all-gather.43.cloned.1.call-start = ((), (), s32[]{:S(2)}) async-start(), calls=%async_computation.22 | async-start | bytes 4456448 | tf_op jit(solution)/shard_map/all_gather | solution.py:88
  11.0 454.5 %reduce-scatter.6.cloned.1.call-start = ((), (), s32[]{:S(2)}) async-start(), calls=%async_computation.5 | async-start | bytes 1310720 | tf_op jit(solution)/shard_map/reduce_scatter | solution.py:133
  11.1 101.5 %copy-start.25 = (f32[2,32,8]{1,2,0:T(8,128)S(1)}, f32[2,32,8]{1,2,0:T(8,128)}, u32[]{:S(2)}) copy-start(f32[2,32,8]{1,2,0:T(8,128)} %param.15) | copy-start | bytes 6148
  11.1 102.5 %copy-start.24 = (s32[2,2,1]{1,2,0:T(1,128)S(1)}, s32[2,2,1]{1,2,0:T(1,128)}, u32[]{:S(2)}) copy-start(s32[2,2,1]{1,2,0:T(1,128)} %param.13) | copy-start | bytes 52
  136.0 99.0 %copy-start.17 = (bf16[1,1,128,4096]{3,2,1,0:T(8,128)(2,1)S(1)}, bf16[1,1,128,4096]{3,2,1,0:T(8,128)(2,1)}, u32[]{:S(2)}) copy-start(bf16[1,1,128,4096]{3,2,1,0:T(8,128)(2,1)} %all-gather.35.cloned.1.call-done) | copy-start | bytes 3145732
  441.8 66.7 %all-gather.21.cloned.1.call-start = ((), (), s32[]{:S(2)}) async-start(), calls=%async_computation.7 | async-start | bytes 1310720 | tf_op jit(solution)/shard_map/all_gather | solution.py:116
  473.0 7.5 collective-permute-start
  481.3 53.2 %all-gather.19.cloned.1.call-start = ((), (), s32[]{:S(2)}) async-start(), calls=%async_computation.6 | async-start | bytes 1310720 | tf_op jit(solution)/shard_map/all_gather | solution.py:117
  481.5 7.4 collective-permute-start.1
  489.6 84.5 %reduce-scatter.8.cloned.1.call-start = ((), (), s32[]{:S(2)}) async-start(), calls=%async_computation.8 | async-start | bytes 1310720 | tf_op jit(solution)/shard_map/reduce_scatter | solution.py:133
  549.5 67.5 %all-gather.25.cloned.1.call-start = ((), (), s32[]{:S(2)}) async-start(), calls=%async_computation.10 | async-start | bytes 1310720 | tf_op jit(solution)/shard_map/all_gather | solution.py:116
  581.6 61.4 %copy-start.28 = (f32[1,4096]{1,0:T(1,128)S(1)}, f32[1,4096]{1,0:T(1,128)}, u32[]{:S(2)}) copy-start(f32[1,4096]{1,0:T(1,128)} %param.16) | copy-start | bytes 49156
  581.6 7.4 collective-permute-start.2
  589.8 53.2 %all-gather.23.cloned.1.call-start = ((), (), s32[]{:S(2)}) async-start(), calls=%async_computation.9 | async-start | bytes 1310720 | tf_op jit(solution)/shard_map/all_gather | solution.py:117
  590.0 7.4 collective-permute-start.3
  598.1 84.5 %reduce-scatter.10.cloned.1.call-start = ((), (), s32[]{:S(2)}) async-start(), calls=%async_computation.11 | async-start | bytes 1310720 | tf_op jit(solution)/shard_map/reduce_scatter | solution.py:133
  658.0 67.5 %all-gather.29.cloned.1.call-start = ((), (), s32[]{:S(2)}) async-start(), calls=%async_computation.13 | async-start | bytes 1310720 | tf_op jit(solution)/shard_map/all_gather | solution.py:116
  690.1 61.3 %copy-start.29 = (f32[1,4096]{1,0:T(1,128)S(1)}, f32[1,4096]{1,0:T(1,128)}, u32[]{:S(2)}) copy-start(f32[1,4096]{1,0:T(1,128)} %param.16) | copy-start | bytes 49156
  690.1 7.5 collective-permute-start.4
  698.3 53.0 %all-gather.27.cloned.1.call-start = ((), (), s32[]{:S(2)}) async-start(), calls=%async_computation.12 | async-start | bytes 1310720 | tf_op jit(solution)/shard_map/all_gather | solution.py:117
  698.6 7.4 collective-permute-start.5
  706.7 84.3 %reduce-scatter.12.cloned.1.call-start = ((), (), s32[]{:S(2)}) async-start(), calls=%async_computation.14 | async-start | bytes 1310720 | tf_op jit(solution)/shard_map/reduce_scatter | solution.py:133
  766.4 67.6 %all-gather.33.cloned.1.call-start = ((), (), s32[]{:S(2)}) async-start(), calls=%async_computation.16 | async-start | bytes 1310720 | tf_op jit(solution)/shard_map/all_gather | solution.py:116
  798.5 61.3 %copy-start.30 = (f32[1,4096]{1,0:T(1,128)S(1)}, f32[1,4096]{1,0:T(1,128)}, u32[]{:S(2)}) copy-start(f32[1,4096]{1,0:T(1,128)} %param.16) | copy-start | bytes 49156
  798.5 7.4 collective-permute-start.6
  806.7 53.0 %all-gather.31.cloned.1.call-start = ((), (), s32[]{:S(2)}) async-start(), calls=%async_computation.15 | async-start | bytes 1310720 | tf_op jit(solution)/shard_map/all_gather | solution.py:117
  806.9 7.4 collective-permute-start.7
  815.1 83.5 %reduce-scatter.14.cloned.1.call-start = ((), (), s32[]{:S(2)}) async-start(), calls=%async_computation.17 | async-start | bytes 1310720 | tf_op jit(solution)/shard_map/reduce_scatter | solution.py:133
  (25 other events, 571.7 us)
Sparse Core Ops, SparseCore 0:
  9.1 27.4 all-gather.34
  39.2 96.7 all-gather.36
  138.6 96.3 all-gather.38
  237.4 96.3 all-gather.40
  336.1 101.6 all-gather.42
  441.9 23.5 reduce-scatter.5
  481.4 27.0 all-gather.20
  510.3 24.0 all-gather.18
  549.6 24.4 reduce-scatter.7
  589.9 27.1 all-gather.24
  618.9 24.0 all-gather.22
  658.1 24.4 reduce-scatter.9
  698.4 27.0 all-gather.28
  727.2 24.0 all-gather.26
  766.5 24.4 reduce-scatter.11
  806.8 27.0 all-gather.32
  835.6 24.0 all-gather.30
  874.1 24.4 reduce-scatter.13
where the time goes:
time: 915 us; the launch traced here: 913 us
  waiting for transfers between devices  628 us (69%)
  local copies, waits for them, and re-layouts  109 us (12%)
  matrix products  71.5 us (8%)
  starting transfers between devices  30 us (3%)
  other arithmetic  27.8 us (3%)
  blocking collectives  25.6 us (3%)
  between operations  20.9 us (2%)
    reduce_scatter x5, waiting for transfers between devices, body(): lax.psum_scatter(partial_value.astype(jnp.bfloat16), 'tensor', scatter_di...  121 us
    gather x1, local copies, waits for them, and re-layouts, positional_bias(): bucket = jnp.take(bucket_row, key_pos - query_pos + (length - 1))  101 us
    all_gather x1, waiting for transfers between devices, body(): lax.all_gather(w_out[0], 'dp', axis=1, tiled=True)  100 us
    all_gather x4, waiting for transfers between devices, body(): lax.all_gather(memory_part, 'tensor', axis=2, tiled=True)  97.3 us
    all_gather x1, waiting for transfers between devices, body(): lax.all_gather(w_key[0], 'dp', axis=0, tiled=True)  95.7 us
    all_gather x1, waiting for transfers between devices, body(): lax.all_gather(w_query[0], 'dp', axis=0, tiled=True)  95.5 us
    all_gather x5, waiting for transfers between devices, body(): lax.all_gather(input_rows, 'tensor', axis=2, tiled=True)  66.7 us
    ppermute x8, waiting for transfers between devices, shifted(): lax.ppermute(value, axis, [(source, source + steps) for source in range(i...  30.5 us
  transfers between devices with their start and end apart: 26, of which 25 were waited for; matrix products, arithmetic and copies ran while one was open for 14% of the time, Pallas kernels for 0%

commit v1 on v0

--- a/solution.py
+++ b/solution.py
@@ -1,3 +1,4 @@
+import functools
 import jax
 import jax.numpy as jnp
 from jax import lax
@@ -5,6 +6,21 @@
 
 D = 4096
 HEAD_DIM = 64
+
+
+def shifts_all_play(u, peer_axis):
+    return jnp.concatenate(
+        lax.all_to_all(
+            jnp.stack([u for _ in range(lax.axis_size(peer_axis))], 0),
+            axis_name=peer_axis,
+            concat_axis=0,
+            split_axis=0,
+        ),
+        axis=1,
+    )
+
+
+_define_corner = functools.partial(shifts_all_play, peer_axis="dp")
 
 
 def shifted(value, axis, steps):
@@ -85,7 +101,7 @@
         lax.all_gather(w_query[0], "dp", axis=0, tiled=True),
         lax.all_gather(w_key[0], "dp", axis=0, tiled=True),
         lax.all_gather(w_value[0], "dp", axis=0, tiled=True),
-        lax.all_gather(w_out[0], "dp", axis=1, tiled=True),
+        _define_corner(w_out[0]),
     )
     score_bias = positional_bias(offset_bucket, bias_tables, section_id, length)
     query_pos = lax.broadcasted_iota(jnp.int32, (length, length), 0)

time: 915 us -> 852 us (0.931)
  waiting for transfers between devices: 628 us -> 550 us
  starting transfers between devices: 30 us -> 41.9 us
    all_gather x1 -> x0, waiting for transfers between devices: 100 us -> none  [body(): lax.all_gather(w_out[0], 'dp', axis=1, tiled=True)]
    all_gather x1, waiting for transfers between devices: 18.8 us -> 95.7 us  [body(): lax.all_gather(w_value[0], 'dp', axis=0, tiled=True)]
    all_gather x1, waiting for transfers between devices: 95.7 us -> 39.8 us  [body(): lax.all_gather(w_key[0], 'dp', axis=0, tiled=True)]
    all_to_all x0 -> x1, starting transfers between devices: none -> 11.9 us  [shifts_all_play(): lax.all_to_all(jnp.stack([u for _ in range(lax.axis_size(peer_axis))], 0)...]
  transfers between devices with their start and end apart: 26 -> 26, of which waited for: 25 -> 24; matrix products, arithmetic and copies ran while one was open for 14% -> 15% of each run, Pallas kernels for 0% -> 0%
where the time goes in v1:
time: 852 us; the launch traced here: 851 us
  waiting for transfers between devices  550 us (65%)
  local copies, waits for them, and re-layouts  113 us (13%)
  matrix products  74 us (9%)
  starting transfers between devices  41.9 us (5%)
  other arithmetic  26.1 us (3%)
  blocking collectives  25.6 us (3%)
  between operations  20.3 us (2%)
    reduce_scatter x5, waiting for transfers between devices, body(): lax.psum_scatter(partial_value.astype(jnp.bfloat16), 'tensor', scatter_di...  121 us
    gather x1, local copies, waits for them, and re-layouts, positional_bias(): bucket = jnp.take(bucket_row, key_pos - query_pos + (length - 1))  101 us
    all_gather x4, waiting for transfers between devices, body(): lax.all_gather(memory_part, 'tensor', axis=2, tiled=True)  97.3 us
    all_gather x1, waiting for transfers between devices, body(): lax.all_gather(w_value[0], 'dp', axis=0, tiled=True)  95.7 us
    all_gather x1, waiting for transfers between devices, body(): lax.all_gather(w_query[0], 'dp', axis=0, tiled=True)  95.2 us
    all_gather x5, waiting for transfers between devices, body(): lax.all_gather(input_rows, 'tensor', axis=2, tiled=True)  68.8 us
    all_gather x1, waiting for transfers between devices, body(): lax.all_gather(w_key[0], 'dp', axis=0, tiled=True)  39.8 us
    ppermute x8, waiting for transfers between devices, shifted(): lax.ppermute(value, axis, [(source, source + steps) for source in range(i...  30.4 us
  transfers between devices with their start and end apart: 26, of which 24 were waited for; matrix products, arithmetic and copies ran while one was open for 15% of the time, Pallas kernels for 0%

profile of v1, /device:TPU:1, one launch (start us, length us, event | category | flops | bytes accessed | tf_op | source)
XLA Modules:
  0.0 850.8 jit_solution(1864489799745352289)
XLA Ops:
  13.8 11.9 %all-to-all-start = ((bf16[16,512,256]{1,2,0:T(8,128)(2,1)}), bf16[16,512,256]{1,2,0:T(8,128)(2,1)}, u32[]{:S(2)}, u32[]{:S(2)}) async-start(bf16[16,512,256]{1,2,0:T(8,128)(2,1)} %stack.3), calls=%async_computation | async-start | bytes 8388608 | tf_op jit(solution)/shard_map/all_to_all | solution.py:13
  25.9 101.4 %gather_fusion = s32[16384]{0:T(1024)S(1)} fusion(s32[255]{0:T(256)S(1)} %bitcast.317, s32[16384]{0:T(1024)S(1)} %fusion.167), kind=kCustom, calls=%fused_computation | custom fusion | bytes 196608 | tf_op jit(solution)/shard_map/jit(_take)/gather | solution.py:38
  131.8 39.8 %all-gather.39.cloned.1.call-done = bf16[1,4096,512]{2,1,0:T(8,128)(2,1)} async-done(((bf16[1,256,512]{2,1,0:T(8,128)(2,1)}), bf16[1,4096,512]{2,1,0:T(8,128)(2,1)}) %all-gather.39.cloned.1.call-update) | async-done | bytes 4194320 | tf_op jit(solution)/shard_map/all_gather | solution.py:102
  175.0 95.2 %all-gather.37.cloned.1.call-done = bf16[1,4096,512]{2,1,0:T(8,128)(2,1)} async-done(((bf16[1,256,512]{2,1,0:T(8,128)(2,1)}), bf16[1,4096,512]{2,1,0:T(8,128)(2,1)}) %all-gather.37.cloned.1.call-update) | async-done | bytes 4194320 | tf_op jit(solution)/shard_map/all_gather | solution.py:101
  273.3 95.7 %all-gather.35.cloned.1.call-done = bf16[1,4096,512]{2,1,0:T(8,128)(2,1)} async-done(((bf16[1,256,512]{2,1,0:T(8,128)(2,1)}), bf16[1,4096,512]{2,1,0:T(8,128)(2,1)}) %all-gather.35.cloned.1.call-update) | async-done | bytes 4194320 | tf_op jit(solution)/shard_map/all_gather | solution.py:103
  372.9 4.7 fusion.5
  377.7 23.6 %reduce-scatter.6.cloned.1.call-done = bf16[1,128,1024]{2,1,0:T(8,128)(2,1)} async-done(((bf16[1,128,4096]{2,1,0:T(8,128)(2,1)}), bf16[1,128,1024]{2,1,0:T(8,128)(2,1)}) %reduce-scatter.6.cloned.1.call-update) | async-done | bytes 262160 | tf_op jit(solution)/shard_map/reduce_scatter | solution.py:149
  402.5 5.1 psum.35
  411.9 4.3 collective-permute-done
  427.4 16.9 %all-gather.19.cloned.1.call-done = bf16[1,128,4096]{2,1,0:T(8,128)(2,1)} async-done(((bf16[1,128,1024]{2,1,0:T(8,128)(2,1)}), bf16[1,128,4096]{2,1,0:T(8,128)(2,1)}) %all-gather.19.cloned.1.call-update) | async-done | bytes 1048592 | tf_op jit(solution)/shard_map/all_gather | solution.py:132
  445.9 24.4 %all-gather.17.cloned.1.call-done = bf16[1,128,4096]{2,1,0:T(8,128)(2,1)} async-done(((bf16[1,128,1024]{2,1,0:T(8,128)(2,1)}), bf16[1,128,4096]{2,1,0:T(8,128)(2,1)}) %all-gather.17.cloned.1.call-update) | async-done | bytes 1048592 | tf_op jit(solution)/shard_map/all_gather | solution.py:133
  480.9 4.7 fusion.6
  485.7 24.5 %reduce-scatter.8.cloned.1.call-done = bf16[1,128,1024]{2,1,0:T(8,128)(2,1)} async-done(((bf16[1,128,4096]{2,1,0:T(8,128)(2,1)}), bf16[1,128,1024]{2,1,0:T(8,128)(2,1)}) %reduce-scatter.8.cloned.1.call-update) | async-done | bytes 262160 | tf_op jit(solution)/shard_map/reduce_scatter | solution.py:149
  511.4 5.1 psum.36
  535.5 17.7 %all-gather.23.cloned.1.call-done = bf16[1,128,4096]{2,1,0:T(8,128)(2,1)} async-done(((bf16[1,128,1024]{2,1,0:T(8,128)(2,1)}), bf16[1,128,4096]{2,1,0:T(8,128)(2,1)}) %all-gather.23.cloned.1.call-update) | async-done | bytes 1048592 | tf_op jit(solution)/shard_map/all_gather | solution.py:132
  554.7 24.3 %all-gather.21.cloned.1.call-done = bf16[1,128,4096]{2,1,0:T(8,128)(2,1)} async-done(((bf16[1,128,1024]{2,1,0:T(8,128)(2,1)}), bf16[1,128,4096]{2,1,0:T(8,128)(2,1)}) %all-gather.21.cloned.1.call-update) | async-done | bytes 1048592 | tf_op jit(solution)/shard_map/all_gather | solution.py:133
  589.6 4.7 fusion.7
  594.4 24.5 %reduce-scatter.10.cloned.1.call-done = bf16[1,128,1024]{2,1,0:T(8,128)(2,1)} async-done(((bf16[1,128,4096]{2,1,0:T(8,128)(2,1)}), bf16[1,128,1024]{2,1,0:T(8,128)(2,1)}) %reduce-scatter.10.cloned.1.call-update) | async-done | bytes 262160 | tf_op jit(solution)/shard_map/reduce_scatter | solution.py:149
  620.1 5.2 psum.37
  629.5 4.3 collective-permute-done.4
  644.9 17.0 %all-gather.27.cloned.1.call-done = bf16[1,128,4096]{2,1,0:T(8,128)(2,1)} async-done(((bf16[1,128,1024]{2,1,0:T(8,128)(2,1)}), bf16[1,128,4096]{2,1,0:T(8,128)(2,1)}) %all-gather.27.cloned.1.call-update) | async-done | bytes 1048592 | tf_op jit(solution)/shard_map/all_gather | solution.py:132
  663.5 24.4 %all-gather.25.cloned.1.call-done = bf16[1,128,4096]{2,1,0:T(8,128)(2,1)} async-done(((bf16[1,128,1024]{2,1,0:T(8,128)(2,1)}), bf16[1,128,4096]{2,1,0:T(8,128)(2,1)}) %all-gather.25.cloned.1.call-update) | async-done | bytes 1048592 | tf_op jit(solution)/shard_map/all_gather | solution.py:133
  698.5 4.7 fusion.8
  703.3 24.5 %reduce-scatter.12.cloned.1.call-done = bf16[1,128,1024]{2,1,0:T(8,128)(2,1)} async-done(((bf16[1,128,4096]{2,1,0:T(8,128)(2,1)}), bf16[1,128,1024]{2,1,0:T(8,128)(2,1)}) %reduce-scatter.12.cloned.1.call-update) | async-done | bytes 262160 | tf_op jit(solution)/shard_map/reduce_scatter | solution.py:149
  729.0 5.1 psum.38
  738.4 4.4 collective-permute-done.6
  743.8 4.1 collective-permute-start.7
  753.7 17.1 %all-gather.31.cloned.1.call-done = bf16[1,128,4096]{2,1,0:T(8,128)(2,1)} async-done(((bf16[1,128,1024]{2,1,0:T(8,128)(2,1)}), bf16[1,128,4096]{2,1,0:T(8,128)(2,1)}) %all-gather.31.cloned.1.call-update) | async-done | bytes 1048592 | tf_op jit(solution)/shard_map/all_gather | solution.py:132
  772.3 24.3 %all-gather.29.cloned.1.call-done = bf16[1,128,4096]{2,1,0:T(8,128)(2,1)} async-done(((bf16[1,128,1024]{2,1,0:T(8,128)(2,1)}), bf16[1,128,4096]{2,1,0:T(8,128)(2,1)}) %all-gather.29.cloned.1.call-update) | async-done | bytes 1048592 | tf_op jit(solution)/shard_map/all_gather | solution.py:133
  806.9 4.7 fusion.9
  812.4 23.8 %reduce-scatter.14.cloned.1.call-done = bf16[1,128,1024]{2,1,0:T(8,128)(2,1)} async-done(((bf16[1,128,4096]{2,1,0:T(8,128)(2,1)}), bf16[1,128,1024]{2,1,0:T(8,128)(2,1)}) %reduce-scatter.14.cloned.1.call-update) | async-done | bytes 262160 | tf_op jit(solution)/shard_map/reduce_scatter | solution.py:149
  837.3 5.1 psum.39
  (204 shorter events, 133.2 us)
Async XLA Ops:
  6.5 123.7 %all-gather.33.cloned.1.call-start = ((), (), s32[]{:S(2)}) async-start(), calls=%async_computation.19 | async-start | bytes 1310720 | tf_op jit(solution)/shard_map/all_gather | solution.py:132
  8.3 163.2 %all-gather.39.cloned.1.call-start = ((), (), s32[]{:S(2)}) async-start(), calls=%async_computation.22 | async-start | bytes 4456448 | tf_op jit(solution)/shard_map/all_gather | solution.py:102
  9.1 261.2 %all-gather.37.cloned.1.call-start = ((), (), s32[]{:S(2)}) async-start(), calls=%async_computation.21 | async-start | bytes 4456448 | tf_op jit(solution)/shard_map/all_gather | solution.py:101
  9.8 359.3 %all-gather.35.cloned.1.call-start = ((), (), s32[]{:S(2)}) async-start(), calls=%async_computation.20 | async-start | bytes 4456448 | tf_op jit(solution)/shard_map/all_gather | solution.py:103
  13.8 359.0 %all-to-all-start = ((bf16[16,512,256]{1,2,0:T(8,128)(2,1)}), bf16[16,512,256]{1,2,0:T(8,128)(2,1)}, u32[]{:S(2)}, u32[]{:S(2)}) async-start(bf16[16,512,256]{1,2,0:T(8,128)(2,1)} %stack.3), calls=%async_computation | async-start | bytes 8388608 | tf_op jit(solution)/shard_map/all_to_all | solution.py:13
  25.7 375.6 %reduce-scatter.6.cloned.1.call-start = ((), (), s32[]{:S(2)}) async-start(), calls=%async_computation.6 | async-start | bytes 1310720 | tf_op jit(solution)/shard_map/reduce_scatter | solution.py:149
  25.9 101.5 %copy-start.25 = (f32[2,32,8]{1,2,0:T(8,128)S(1)}, f32[2,32,8]{1,2,0:T(8,128)}, u32[]{:S(2)}) copy-start(f32[2,32,8]{1,2,0:T(8,128)} %param.15) | copy-start | bytes 6148
  25.9 102.4 %copy-start.24 = (s32[2,2,1]{1,2,0:T(1,128)S(1)}, s32[2,2,1]{1,2,0:T(1,128)}, u32[]{:S(2)}) copy-start(s32[2,2,1]{1,2,0:T(1,128)} %param.13) | copy-start | bytes 52
  127.3 44.2 %copy-start.27 = (f32[1,4096]{1,0:T(1,128)S(1)}, f32[1,4096]{1,0:T(1,128)}, u32[]{:S(2)}) copy-start(f32[1,4096]{1,0:T(1,128)} %param.16) | copy-start | bytes 49156
  171.5 98.7 %copy-start.17 = (bf16[1,1,128,4096]{3,2,1,0:T(8,128)(2,1)S(1)}, bf16[1,1,128,4096]{3,2,1,0:T(8,128)(2,1)}, u32[]{:S(2)}) copy-start(bf16[1,1,128,4096]{3,2,1,0:T(8,128)(2,1)} %all-gather.33.cloned.1.call-done) | copy-start | bytes 3145732
  377.6 66.7 %all-gather.19.cloned.1.call-start = ((), (), s32[]{:S(2)}) async-start(), calls=%async_computation.8 | async-start | bytes 1310720 | tf_op jit(solution)/shard_map/all_gather | solution.py:132
  408.8 7.4 collective-permute-start
  417.0 53.2 %all-gather.17.cloned.1.call-start = ((), (), s32[]{:S(2)}) async-start(), calls=%async_computation.7 | async-start | bytes 1310720 | tf_op jit(solution)/shard_map/all_gather | solution.py:133
  417.2 7.4 collective-permute-start.1
  425.4 84.9 %reduce-scatter.8.cloned.1.call-start = ((), (), s32[]{:S(2)}) async-start(), calls=%async_computation.9 | async-start | bytes 1310720 | tf_op jit(solution)/shard_map/reduce_scatter | solution.py:149
  485.6 40.3 %copy-start.14 = (bf16[1,128,1024]{2,1,0:T(8,128)(2,1)S(1)}, bf16[1,128,1024]{2,1,0:T(8,128)(2,1)}, u32[]{:S(2)}) copy-start(bf16[1,128,1024]{2,1,0:T(8,128)(2,1)} %copy-done.13) | copy-start | bytes 786436
  485.6 67.6 %all-gather.23.cloned.1.call-start = ((), (), s32[]{:S(2)}) async-start(), calls=%async_computation.11 | async-start | bytes 1310720 | tf_op jit(solution)/shard_map/all_gather | solution.py:132
  517.7 7.4 collective-permute-start.2
  525.9 53.1 %all-gather.21.cloned.1.call-start = ((), (), s32[]{:S(2)}) async-start(), calls=%async_computation.10 | async-start | bytes 1310720 | tf_op jit(solution)/shard_map/all_gather | solution.py:133
  526.1 7.4 collective-permute-start.3
  534.2 84.7 %reduce-scatter.10.cloned.1.call-start = ((), (), s32[]{:S(2)}) async-start(), calls=%async_computation.12 | async-start | bytes 1310720 | tf_op jit(solution)/shard_map/reduce_scatter | solution.py:149
  594.4 67.6 %all-gather.27.cloned.1.call-start = ((), (), s32[]{:S(2)}) async-start(), calls=%async_computation.14 | async-start | bytes 1310720 | tf_op jit(solution)/shard_map/all_gather | solution.py:132
  626.4 7.4 collective-permute-start.4
  634.6 53.3 %all-gather.25.cloned.1.call-start = ((), (), s32[]{:S(2)}) async-start(), calls=%async_computation.13 | async-start | bytes 1310720 | tf_op jit(solution)/shard_map/all_gather | solution.py:133
  634.8 7.4 collective-permute-start.5
  643.0 84.9 %reduce-scatter.12.cloned.1.call-start = ((), (), s32[]{:S(2)}) async-start(), calls=%async_computation.15 | async-start | bytes 1310720 | tf_op jit(solution)/shard_map/reduce_scatter | solution.py:149
  703.2 40.4 %copy-start.12 = (bf16[1,128,1024]{2,1,0:T(8,128)(2,1)S(1)}, bf16[1,128,1024]{2,1,0:T(8,128)(2,1)}, u32[]{:S(2)}) copy-start(bf16[1,128,1024]{2,1,0:T(8,128)(2,1)} %copy-done.11) | copy-start | bytes 786436
  703.2 67.6 %all-gather.31.cloned.1.call-start = ((), (), s32[]{:S(2)}) async-start(), calls=%async_computation.17 | async-start | bytes 1310720 | tf_op jit(solution)/shard_map/all_gather | solution.py:132
  735.3 7.5 collective-permute-start.6
  743.6 53.0 %all-gather.29.cloned.1.call-start = ((), (), s32[]{:S(2)}) async-start(), calls=%async_computation.16 | async-start | bytes 1310720 | tf_op jit(solution)/shard_map/all_gather | solution.py:133
  743.8 7.6 collective-permute-start.7
  752.2 84.0 %reduce-scatter.14.cloned.1.call-start = ((), (), s32[]{:S(2)}) async-start(), calls=%async_computation.18 | async-start | bytes 1310720 | tf_op jit(solution)/shard_map/reduce_scatter | solution.py:149
  (22 other events, 477.7 us)
Sparse Core Ops, SparseCore 0:
  9.1 44.6 all-gather.32
  56.4 115.0 all-gather.38
  174.1 96.0 all-gather.36
  272.7 96.3 all-gather.34
  377.8 23.5 reduce-scatter.5
  417.2 27.1 all-gather.18
  446.1 24.0 all-gather.16
  485.7 24.4 reduce-scatter.7
  526.0 27.1 all-gather.22
  554.9 24.0 all-gather.20
  594.5 24.3 reduce-scatter.9
  634.7 27.1 all-gather.26
  663.7 24.0 all-gather.24
  703.3 24.4 reduce-scatter.11
  743.7 27.0 all-gather.30
  772.5 24.0 all-gather.28
  811.7 24.4 reduce-scatter.13
